TPU v7x, 32 devices: a whole 2x2x4 slice. The times are simulated.
32 devices in a mesh: sec: 2 (over x), blk: 8 (over z, y), mp: 2 (over core).
Axes of the slice: x: 2, y: 2, z: 4, core: 2. Of those that a mesh axis runs over, the one named last changes fastest.
Arguments:
- image_pooled: bfloat16 [1536, 1536], P('blk', ('sec', 'mp')), may hold values from -4 to 4
- text_pooled: bfloat16 [1536, 2048], P('blk', ('sec', 'mp')), may hold values from -4 to 4
- image_proj: bfloat16 [1536, 1152], P(('sec', 'mp')), may hold values from -0.15625 to 0.15625
- text_proj: bfloat16 [2048, 1152], P(('sec', 'mp')), may hold values from -0.125 to 0.125
- natural_log_multiplier: float32 [1], replicated, may hold values from 1.4 to 2.3
- logit_bias: float32 [1], replicated, may hold values from -2 to -0.5
- match_cluster_labels: int32 [1536], P('blk'), may hold values from 0 to 1535
Outputs:
- pair_loss: float32 [2, 1536], P('sec', 'blk')
- image_grad: bfloat16 [1536, 1536], P('blk', ('sec', 'mp'))
- text_grad: bfloat16 [1536, 2048], P('blk', ('sec', 'mp'))
All inputs are finite; a program needn't handle non-finite values.
Results may differ from a plain program's by a relative error of at most 0.0065.
Values may be sent and summed in bfloat16 or wider, within the bound.
No kernel may reach another device: no remote copies, remote signals or barrier semaphores. Data moves between devices by JAX's collectives and lax.ppermute only.
A program may use at most 128 MiB of HBM per device.

v0:
```python
import jax
import jax.numpy as jnp
from jax import lax
from jax.sharding import PartitionSpec as P


def unit_rows(embedding):
    row_norm = jnp.sqrt(jnp.sum(embedding * embedding, axis=1, keepdims=True) + 1e-06)
    return (embedding / row_norm, row_norm)


def per_device(
    image_pooled,
    text_pooled,
    image_proj,
    text_proj,
    natural_log_multiplier,
    logit_bias,
    match_cluster_labels,
):
    part_image = jnp.dot(image_pooled, image_proj, preferred_element_type=jnp.float32)
    part_text = jnp.dot(text_pooled, text_proj, preferred_element_type=jnp.float32)
    stacked = jnp.stack([part_image, part_text])
    section = lax.axis_index("sec")
    both_sums = lax.psum(stacked, ("sec", "mp"))
    own_emb = lax.dynamic_index_in_dim(both_sums, section, 0, keepdims=False)
    other_emb = lax.dynamic_index_in_dim(both_sums, 1 - section, 0, keepdims=False)
    own_unit, own_norm = unit_rows(own_emb)
    resident_slice = own_unit.astype(jnp.bfloat16)
    other_unit, other_norm = unit_rows(other_emb)
    counterpart_slice = other_unit.astype(jnp.bfloat16)
    sharpness_factor = jnp.exp(natural_log_multiplier[0])
    shift_quantity = logit_bias[0]
    visit_rows = lax.all_gather(counterpart_slice, "blk", axis=0, tiled=True)
    visited_ids = lax.all_gather(match_cluster_labels, "blk", axis=0, tiled=True)
    agreement_scores_matrix = (
        sharpness_factor
        * lax.dot_general(
            resident_slice, visit_rows, (((1,), (1,)), ((), ())), preferred_element_type=jnp.float32
        )
        + shift_quantity
    )
    desired_polarity = jnp.where(
        match_cluster_labels[:, None] == visited_ids[None, :], 1.0, -1.0
    ).astype(jnp.float32)
    row_losses = jnp.sum(jax.nn.softplus(-desired_polarity * agreement_scores_matrix), axis=1)
    penalty_factor = (
        -sharpness_factor
        * desired_polarity
        * jax.nn.sigmoid(-desired_polarity * agreement_scores_matrix)
    ).astype(jnp.bfloat16)
    unit_grad = jnp.dot(penalty_factor, visit_rows, preferred_element_type=jnp.float32)
    unit_grad, row_losses = (unit_grad, row_losses)
    projection = jnp.sum(own_unit * unit_grad, axis=1, keepdims=True)
    own_demb = ((unit_grad - own_unit * projection) / own_norm).astype(jnp.bfloat16)
    both_grads = lax.all_gather(own_demb[None], "sec", axis=0, tiled=True)
    image_grad = lax.dot_general(
        both_grads[0], image_proj, (((1,), (1,)), ((), ())), preferred_element_type=jnp.float32
    ).astype(jnp.bfloat16)
    text_grad = lax.dot_general(
        both_grads[1], text_proj, (((1,), (1,)), ((), ())), preferred_element_type=jnp.float32
    ).astype(jnp.bfloat16)
    return (row_losses[None, :], image_grad, text_grad)


def solution(mesh):
    placed = (
        P("blk", ("sec", "mp")),
        P("blk", ("sec", "mp")),
        P(("sec", "mp"), None),
        P(("sec", "mp"), None),
        P(),
        P(),
        P("blk"),
    )
    return jax.shard_map(
        per_device,
        mesh=mesh,
        in_specs=placed,
        out_specs=(P("sec", "blk"), P("blk", ("sec", "mp")), P("blk", ("sec", "mp"))),
        check_vma=False,
    )
```

profile of v0, /device:TPU:0, one launch (start us, length us, event | category | flops | bytes accessed | tf_op | source)
XLA Modules:
  0.0 155.9 jit_solution(17890607806463199969)
XLA Ops:
  7.2 0.0 copy-start
  7.2 0.0 copy-start.4
  7.2 0.0 copy-start.2
  7.2 0.0 all-reduce.3.cloned.1.call-start
  7.2 1.2 copy-done
  8.4 1.4 convolution_bitcast_fusion
  9.8 0.0 copy-done.4
  9.8 0.0 copy-done.2
  9.8 0.4 convolution_bitcast_fusion.1
  10.2 1.3 pad_maximum_fusion
  11.6 0.0 all-reduce.3.cloned.1.call-update
  11.6 0.0 all-gather.3.cloned.1.call-start
  11.6 48.8 %all-reduce.3.cloned.1.call-done = f32[2,192,1152]{2,1,0:T(8,128)} async-done(((f32[2,192,1152]{2,1,0:T(8,128)}), f32[2,192,1152]{2,1,0:T(8,128)}) %all-reduce.3.cloned.1.call-update) | async-done | bytes 1769488 | tf_op jit(solution)/shard_map/psum | solution.py:25
  60.5 0.0 copy-start.1
  60.5 1.8 %fusion.7 = (f32[192]{0:T(256)S(1)}, f32[192]{0:T(256)S(1)}) fusion(f32[2,192,1152]{2,1,0:T(8,128)} %all-reduce.3.cloned.1.call-done, s32[]{:T(128)S(6)} %select_n.16, s32[]{:T(128)S(6)} %select_n.17), kind=kLoop, calls=%fused_computation.20 | loop fusion | flops 884352 | bytes 1771016 | tf_op jit(solution)/shard_map/reduce_sum | solution.py:8
  62.2 0.0 copy-start.7
  62.3 0.0 copy-start.5
  62.3 0.2 copy-done.1
  62.5 0.9 fusion.6
  63.4 0.0 all-gather.3.cloned.1.call-update
  64.7 0.0 copy-done.7
  64.8 0.6 dynamic-slice
  66.0 0.0 copy-done.5
  66.0 0.3 dynamic-update-slice
  66.3 12.1 %all-reduce = s32[1536]{0:T(1024)S(1)} all-reduce(s32[1536]{0:T(1024)S(1)} %dynamic-update-slice), channel_id=1, replica_groups=mesh['sec'=2,'blk'=8,'mp'=2] {'blk'}, use_global_device_ids=true, to_apply=%add | all-reduce | flops 1536 | bytes 12288
  78.4 50.5 %all-gather.3.cloned.1.call-done = bf16[1536,1152]{1,0:T(8,128)(2,1)} async-done(((bf16[192,1152]{1,0:T(8,128)(2,1)}), bf16[1536,1152]{1,0:T(8,128)(2,1)}) %all-gather.3.cloned.1.call-update) | async-done | bytes 3538960 | tf_op jit(solution)/shard_map/all_gather | solution.py:34
  128.9 0.0 copy-start.6
  128.9 4.7 %fusion.4 = (f32[192]{0:T(256)}, f32[192,1536]{1,0:T(8,128)S(1)}) fusion(f32[]{:T(128)} %bitcast.37, bf16[1536,1152]{1,0:T(8,128)(2,1)} %all-gather.3.cloned.1.call-done, f32[192]{0:T(256)S(1)} %add_sqrt_fusion.1, f32[2,192,1152]{2,1,0:T(8,128)S(1)} %copy-done.1, s32[]{:T(128)S(6)} %select_n.16, f32[]{:T(128)} %bitcast.1, s32[1536]{0:T(1024)S(1)} %all-reduce, ...), kind=kOutput, calls=%fused_computation.11 | convolution fusion | flops 683753280 | bytes 5614348 | tf_op jit(solution)/shard_map/dot_general | solution.py:38
  133.6 0.0 copy-done.6
  133.6 1.1 multiply_reduce_fusion
  134.7 0.2 divide_convert_fusion
  135.0 0.0 copy-start.3
  135.0 11.7 %all-gather = bf16[384,1152]{1,0:T(8,128)(2,1)S(1)} all-gather(bf16[192,1152]{1,0:T(8,128)(2,1)S(1)} %divide_convert_fusion), channel_id=2, replica_groups=mesh['sec'=2,'blk'=8,'mp'=2] {'sec'}, dimensions={0}, use_global_device_ids=true | all-gather | bytes 1327104 | tf_op jit(solution)/shard_map/all_gather | solution.py:56
  146.7 0.0 copy-done.3
  146.7 1.1 convolution_convert_fusion.1
  147.8 1.2 convolution_convert_fusion
  (3 shorter events, 0.0 us)
Async XLA Ops:
  7.2 1.3 copy-start
  7.2 2.6 %copy-start.4 = (bf16[192,384]{1,0:T(8,128)(2,1)S(1)}, bf16[192,384]{1,0:T(8,128)(2,1)}, u32[]{:S(2)}) copy-start(bf16[192,384]{1,0:T(8,128)(2,1)} %param.7) | copy-start | bytes 442372
  7.2 2.6 %copy-start.2 = (bf16[384,1152]{1,0:T(8,128)(2,1)S(1)}, bf16[384,1152]{1,0:T(8,128)(2,1)}, u32[]{:S(2)}) copy-start(bf16[384,1152]{1,0:T(8,128)(2,1)} %param.9) | copy-start | bytes 2654212
  7.2 53.3 %all-reduce.3.cloned.1.call-start = ((), (), s32[]{:S(2)}) async-start(), calls=%async_computation | async-start | bytes 3538944 | tf_op jit(solution)/shard_map/psum | solution.py:25
  11.6 117.3 %all-gather.3.cloned.1.call-start = ((), (), s32[]{:S(2)}) async-start(), calls=%async_computation.1 | async-start | bytes 3981312 | tf_op jit(solution)/shard_map/all_gather | solution.py:34
  60.5 2.0 %copy-start.1 = (f32[2,192,1152]{2,1,0:T(8,128)S(1)}, f32[2,192,1152]{2,1,0:T(8,128)}, u32[]{:S(2)}) copy-start(f32[2,192,1152]{2,1,0:T(8,128)} %all-reduce.3.cloned.1.call-done) | copy-start | bytes 5308420
  62.2 2.5 %copy-start.7 = (u32[32]{0:T(128)S(1)}, u32[32]{0:T(128)}, u32[]{:S(2)}) copy-start(u32[32]{0:T(128)} %constant.31) | copy-start | bytes 388
  62.3 3.8 %copy-start.5 = (s32[192]{0:T(256)S(1)}, s32[192]{0:T(256)}, u32[]{:S(2)}) copy-start(s32[192]{0:T(256)} %param.13) | copy-start | bytes 2308
  128.9 4.7 %copy-start.6 = (bf16[1536,1152]{1,0:T(8,128)(2,1)S(1)}, bf16[1536,1152]{1,0:T(8,128)(2,1)}, u32[]{:S(2)}) copy-start(bf16[1536,1152]{1,0:T(8,128)(2,1)} %all-gather.3.cloned.1.call-done) | copy-start | bytes 10616836
  135.0 11.8 %copy-start.3 = (bf16[384,1152]{1,0:T(8,128)(2,1)S(1)}, bf16[384,1152]{1,0:T(8,128)(2,1)}, u32[]{:S(2)}) copy-start(bf16[384,1152]{1,0:T(8,128)(2,1)} %param.9) | copy-start | bytes 2654212
Sparse Core Ops, SparseCore 0:
  11.7 48.7 all-reduce.2
  63.5 65.3 all-gather.2
where the time goes:
time: 156 us
  waiting for transfers between devices  99.4 us (64%)
  blocking collectives  23.8 us (15%)
  between operations  16.2 us (10%)
  matrix products  9.9 us (6%)
  other arithmetic  4.2 us (3%)
  local copies, waits for them, and re-layouts  2.31 us (1%)
    all_gather x1, waiting for transfers between devices, per_device(): visit_rows = lax.all_gather(counterpart_slice, 'blk', axis=0, tiled=True)  50.5 us
    psum x1, waiting for transfers between devices, per_device(): both_sums = lax.psum(stacked, ('sec', 'mp'))  48.8 us
    unnamed x1, blocking collectives  12.1 us
    all_gather x1, blocking collectives, per_device(): both_grads = lax.all_gather(own_demb[None], 'sec', axis=0, tiled=True)  11.7 us
    dot_general x1, matrix products, per_device(): lax.dot_general(resident_slice, visit_rows, (((1,), (1,)), ((), ())), pre...  4.68 us
  transfers between devices with their start and end apart: 2, of which 2 were waited for; matrix products, arithmetic and copies ran while one was open for 1% of the time, Pallas kernels for 0%

commit v1 on v0

--- a/solution.py
+++ b/solution.py
@@ -22,7 +22,7 @@
     part_text = jnp.dot(text_pooled, text_proj, preferred_element_type=jnp.float32)
     stacked = jnp.stack([part_image, part_text])
     section = lax.axis_index("sec")
-    both_sums = lax.psum(stacked, ("sec", "mp"))
+    both_sums = lax.psum(lax.psum(stacked, "mp"), "sec")
     own_emb = lax.dynamic_index_in_dim(both_sums, section, 0, keepdims=False)
     other_emb = lax.dynamic_index_in_dim(both_sums, 1 - section, 0, keepdims=False)
     own_unit, own_norm = unit_rows(own_emb)

time: 156 us -> 190 us (1.22)
  waiting for transfers between devices: 99.4 us -> 133 us
    psum x1 -> x2, waiting for transfers between devices: 48.8 us -> 82.8 us  [per_device(): both_sums = lax.psum(lax.psum(stacked, 'mp'), 'sec')]
  transfers between devices with their start and end apart: 2 -> 3, of which waited for: 2 -> 3; matrix products, arithmetic and copies ran while one was open for 1% -> 0% of each run, Pallas kernels for 0% -> 0%
where the time goes in v1:
time: 190 us
  waiting for transfers between devices  133 us (70%)
  blocking collectives  23.8 us (13%)
  between operations  15.9 us (8%)
  matrix products  9.9 us (5%)
  other arithmetic  4.2 us (2%)
  local copies, waits for them, and re-layouts  2.31 us (1%)
    psum x2, waiting for transfers between devices, per_device(): both_sums = lax.psum(lax.psum(stacked, 'mp'), 'sec')  82.8 us
    all_gather x1, waiting for transfers between devices, per_device(): visit_rows = lax.all_gather(counterpart_slice, 'blk', axis=0, tiled=True)  50.5 us
    unnamed x1, blocking collectives  12.1 us
    all_gather x1, blocking collectives, per_device(): both_grads = lax.all_gather(own_demb[None], 'sec', axis=0, tiled=True)  11.7 us
    dot_general x1, matrix products, per_device(): lax.dot_general(resident_slice, visit_rows, (((1,), (1,)), ((), ())), pre...  4.68 us
  transfers between devices with their start and end apart: 3, of which 3 were waited for; matrix products, arithmetic and copies ran while one was open for 0% of the time, Pallas kernels for 0%

profile of v1, /device:TPU:0, one launch (start us, length us, event | category | flops | bytes accessed | tf_op | source)
XLA Modules:
  0.0 189.5 jit_solution(14514563013629098337)
XLA Ops:
  7.2 0.0 copy-start
  7.2 0.0 copy-start.4
  7.2 0.0 copy-start.2
  7.2 0.0 all-reduce.4.cloned.1.call-start
  7.2 1.2 copy-done
  8.4 1.4 convolution_bitcast_fusion
  9.8 0.0 copy-done.4
  9.8 0.0 copy-done.2
  9.8 0.4 convolution_bitcast_fusion.1
  10.2 1.3 pad_maximum_fusion
  11.6 0.0 all-reduce.4.cloned.1.call-update
  11.6 0.0 all-reduce.6.cloned.1.call-start
  11.6 23.5 %all-reduce.4.cloned.1.call-done = f32[2,192,1152]{2,1,0:T(8,128)} async-done(((f32[2,192,1152]{2,1,0:T(8,128)}), f32[2,192,1152]{2,1,0:T(8,128)}) %all-reduce.4.cloned.1.call-update) | async-done | bytes 1769488 | tf_op jit(solution)/shard_map/psum | solution.py:25
  35.1 0.0 all-reduce.6.cloned.1.call-update
  35.1 0.0 all-gather.3.cloned.1.call-start
  35.2 59.3 %all-reduce.6.cloned.1.call-done = f32[2,192,1152]{2,1,0:T(8,128)} async-done(((f32[2,192,1152]{2,1,0:T(8,128)}), f32[2,192,1152]{2,1,0:T(8,128)}) %all-reduce.6.cloned.1.call-update) | async-done | bytes 1769488 | tf_op jit(solution)/shard_map/psum | solution.py:25
  94.5 0.0 copy-start.1
  94.5 1.8 fusion.7
  96.3 0.0 copy-start.7
  96.3 0.0 copy-start.5
  96.3 0.2 copy-done.1
  96.5 0.9 fusion.6
  97.4 0.0 all-gather.3.cloned.1.call-update
  98.8 0.0 copy-done.7
  98.8 0.6 dynamic-slice
  100.0 0.0 copy-done.5
  100.0 0.3 dynamic-update-slice
  100.3 12.1 %all-reduce = s32[1536]{0:T(1024)S(1)} all-reduce(s32[1536]{0:T(1024)S(1)} %dynamic-update-slice), channel_id=1, replica_groups=mesh['sec'=2,'blk'=8,'mp'=2] {'blk'}, use_global_device_ids=true, to_apply=%add | all-reduce | flops 1536 | bytes 12288
  112.4 50.5 %all-gather.3.cloned.1.call-done = bf16[1536,1152]{1,0:T(8,128)(2,1)} async-done(((bf16[192,1152]{1,0:T(8,128)(2,1)}), bf16[1536,1152]{1,0:T(8,128)(2,1)}) %all-gather.3.cloned.1.call-update) | async-done | bytes 3538960 | tf_op jit(solution)/shard_map/all_gather | solution.py:34
  162.9 0.0 copy-start.6
  162.9 4.7 %fusion.4 = (f32[192]{0:T(256)}, f32[192,1536]{1,0:T(8,128)S(1)}) fusion(f32[]{:T(128)} %bitcast.37, bf16[1536,1152]{1,0:T(8,128)(2,1)} %all-gather.3.cloned.1.call-done, f32[192]{0:T(256)S(1)} %add_sqrt_fusion.1, f32[2,192,1152]{2,1,0:T(8,128)S(1)} %copy-done.1, s32[]{:T(128)S(6)} %select_n.16, f32[]{:T(128)} %bitcast.1, s32[1536]{0:T(1024)S(1)} %all-reduce, ...), kind=kOutput, calls=%fused_computation.11 | convolution fusion | flops 683753280 | bytes 5614348 | tf_op jit(solution)/shard_map/dot_general | solution.py:38
  167.5 0.0 copy-done.6
  167.6 1.1 multiply_reduce_fusion
  168.7 0.2 divide_convert_fusion
  168.9 0.0 copy-start.3
  168.9 11.7 %all-gather = bf16[384,1152]{1,0:T(8,128)(2,1)S(1)} all-gather(bf16[192,1152]{1,0:T(8,128)(2,1)S(1)} %divide_convert_fusion), channel_id=2, replica_groups=mesh['sec'=2,'blk'=8,'mp'=2] {'sec'}, dimensions={0}, use_global_device_ids=true | all-gather | bytes 1327104 | tf_op jit(solution)/shard_map/all_gather | solution.py:56
  180.7 0.0 copy-done.3
  180.7 1.1 convolution_convert_fusion.1
  181.8 1.2 convolution_convert_fusion
  (3 shorter events, 0.0 us)
Async XLA Ops:
  7.2 1.3 copy-start
  7.2 2.6 %copy-start.4 = (bf16[192,384]{1,0:T(8,128)(2,1)S(1)}, bf16[192,384]{1,0:T(8,128)(2,1)}, u32[]{:S(2)}) copy-start(bf16[192,384]{1,0:T(8,128)(2,1)} %param.7) | copy-start | bytes 442372
  7.2 2.6 %copy-start.2 = (bf16[384,1152]{1,0:T(8,128)(2,1)S(1)}, bf16[384,1152]{1,0:T(8,128)(2,1)}, u32[]{:S(2)}) copy-start(bf16[384,1152]{1,0:T(8,128)(2,1)} %param.9) | copy-start | bytes 2654212
  7.2 27.9 %all-reduce.4.cloned.1.call-start = ((), (), s32[]{:S(2)}) async-start(), calls=%async_computation | async-start | bytes 3538944 | tf_op jit(solution)/shard_map/psum | solution.py:25
  11.6 82.9 %all-reduce.6.cloned.1.call-start = ((), (), s32[]{:S(2)}) async-start(), calls=%async_computation.1 | async-start | bytes 3538944 | tf_op jit(solution)/shard_map/psum | solution.py:25
  35.1 127.7 %all-gather.3.cloned.1.call-start = ((), (), s32[]{:S(2)}) async-start(), calls=%async_computation.2 | async-start | bytes 3981312 | tf_op jit(solution)/shard_map/all_gather | solution.py:34
  94.5 2.0 %copy-start.1 = (f32[2,192,1152]{2,1,0:T(8,128)S(1)}, f32[2,192,1152]{2,1,0:T(8,128)}, u32[]{:S(2)}) copy-start(f32[2,192,1152]{2,1,0:T(8,128)} %all-reduce.6.cloned.1.call-done) | copy-start | bytes 5308420
  96.3 2.5 %copy-start.7 = (u32[32]{0:T(128)S(1)}, u32[32]{0:T(128)}, u32[]{:S(2)}) copy-start(u32[32]{0:T(128)} %constant.31) | copy-start | bytes 388
  96.3 3.8 %copy-start.5 = (s32[192]{0:T(256)S(1)}, s32[192]{0:T(256)}, u32[]{:S(2)}) copy-start(s32[192]{0:T(256)} %param.13) | copy-start | bytes 2308
  162.9 4.7 %copy-start.6 = (bf16[1536,1152]{1,0:T(8,128)(2,1)S(1)}, bf16[1536,1152]{1,0:T(8,128)(2,1)}, u32[]{:S(2)}) copy-start(bf16[1536,1152]{1,0:T(8,128)(2,1)} %all-gather.3.cloned.1.call-done) | copy-start | bytes 10616836
  168.9 11.8 %copy-start.3 = (bf16[384,1152]{1,0:T(8,128)(2,1)S(1)}, bf16[384,1152]{1,0:T(8,128)(2,1)}, u32[]{:S(2)}) copy-start(bf16[384,1152]{1,0:T(8,128)(2,1)} %param.9) | copy-start | bytes 2654212
Sparse Core Ops, SparseCore 0:
  11.7 23.3 all-reduce.3
  37.5 56.9 all-reduce.5
  97.5 65.2 all-gather.2
